TPU v7x, 32 devices: a whole 2x2x4 slice. The times are simulated.
32 devices in a mesh: groups: 2 (over y), seq: 4 (over z), adapt: 4 (over x, core).
Axes of the slice: x: 2, y: 2, z: 4, core: 2. Of those that a mesh axis runs over, the one named last changes fastest.
Arguments:
- image: bfloat16 [16, 2048, 3072], P(('groups', 'adapt'), 'seq'), parts along dimension 0, may hold values from -6 to 6
- modulation: float32 [16, 2, 3072], P(('groups', 'adapt')), parts along dimension 0, may hold values from -3 to 3
- query_key_value_weight: bfloat16 [3072, 6144], P(None, 'adapt'), may hold values from -0.109375 to 0.109375
- pooled_down_factor: bfloat16 [16, 3072, 64], P('seq'), may hold values from -0.109375 to 0.109375
- pooled_up_factor: bfloat16 [16, 64, 6144], P('seq', None, 'adapt'), may hold values from -0.75 to 0.75
- request_adapter: int32 [16], P('groups'), parts along dimension 0, may hold values from 0 to 15
- adapter_slot_table: int32 [16], replicated, may hold values from 0 to 15, each once
- row_request: int32 [16], P('groups'), parts along dimension 0, may hold values from 0 to 7, each once
- text_key_value: bfloat16 [16, 512, 2, 2048], P('groups', 'seq', None, 'adapt'), parts along dimension 0, may hold values from -110 to 110
- query_key_gain: float32 [2, 128], replicated, may hold values from 1 to 2.5
Outputs:
- attended: bfloat16 [16, 2048, 2048], P('groups', 'seq', 'adapt'), parts along dimension 0
There are 2 independent parts, one for each index of `groups`. A program takes and returns all parts, laid end to end along the dimension named above; an argument that names none is the same for every part. Nothing has to cross between parts.
All inputs are finite; a program needn't handle non-finite values.
Results may differ from a plain program's by a relative error of at most 0.0049.
The roundings to bfloat16 on the way count: a program that leaves them out, or rounds other values in their place, can miss the bound.
Values may be sent and summed in bfloat16 or wider, within the bound.
A program may use at most 192 MiB of HBM per device.

v0:
```python
import math
import jax
import jax.numpy as jnp
from jax import lax
from jax.sharding import PartitionSpec as P

HEAD_SIZE = 128


def layer_modulate(image, modulation):
    widened = image.astype(jnp.float32)
    centre = widened - jnp.mean(widened, axis=-1, keepdims=True)
    variance = jnp.mean(centre * centre, axis=-1, keepdims=True)
    normed = centre * lax.rsqrt(variance + 1e-06)
    return ((1.0 + modulation[:, 1, None, :]) * normed + modulation[:, 0, None, :]).astype(
        jnp.bfloat16
    )


def rms_scale(values, gain):
    return values * lax.rsqrt(jnp.mean(values * values, axis=-1, keepdims=True) + 1e-06) * gain


def attend_item(operands):
    queries, joined = operands
    key_rows = joined[:, 0]
    value_rows = joined[:, 1]
    query_count = queries.shape[0]
    block = math.gcd(query_count, 512)
    inverse = 1.0 / math.sqrt(queries.shape[-1])
    blocked = queries.reshape(query_count // block, block, queries.shape[-1])

    def one_block(block_rows):
        scores = (
            lax.dot_general(
                block_rows, key_rows, (((1,), (1,)), ((), ())), preferred_element_type=jnp.float32
            )
            * inverse
        )
        highest = jnp.max(scores, axis=-1, keepdims=True)
        weights = jnp.exp(scores - highest)
        weights = weights / jnp.sum(weights, axis=-1, keepdims=True)
        return jnp.dot(
            weights.astype(jnp.bfloat16), value_rows, preferred_element_type=jnp.float32
        ).astype(jnp.bfloat16)

    return lax.map(one_block, blocked).reshape(queries.shape)


def on_device(
    image,
    modulation,
    query_key_value_weight,
    pooled_down_factor,
    pooled_up_factor,
    request_adapter,
    adapter_slot_table,
    row_request,
    text_key_value,
    query_key_gain,
):
    seq_index = lax.axis_index("seq")
    all_requests = request_adapter.shape[0]
    local_pool_slice = pooled_down_factor.shape[0]
    pool_total = adapter_slot_table.shape[0]
    heads_local = query_key_value_weight.shape[1] // (3 * HEAD_SIZE)
    text_local = text_key_value.shape[1]
    modulated = layer_modulate(image, modulation)
    request_match = row_request[:, None] == jnp.arange(all_requests, dtype=jnp.int32)[None, :]
    chosen_ids = jnp.sum(jnp.where(request_match, request_adapter[None, :], 0), axis=1)
    slot_match = chosen_ids[:, None] == jnp.arange(pool_total, dtype=jnp.int32)[None, :]
    slots = jnp.sum(jnp.where(slot_match, adapter_slot_table[None, :], 0), axis=1)
    owned = slots // local_pool_slice == seq_index
    local_match = (slots % local_pool_slice)[:, None] == jnp.arange(
        local_pool_slice, dtype=jnp.int32
    )[None, :]
    slot_picker = (owned[:, None] & local_match).astype(jnp.bfloat16)
    up_terms = jnp.einsum(
        "eq,qfx->efx", slot_picker, pooled_up_factor, preferred_element_type=jnp.float32
    ).astype(jnp.bfloat16)
    down_terms = jnp.einsum(
        "mv,vna->mna", slot_picker, pooled_down_factor, preferred_element_type=jnp.float32
    ).astype(jnp.bfloat16)
    down_fetched, up_fetched = (
        lax.psum(down_terms, "seq").astype(jnp.float32),
        lax.psum(up_terms, "seq").astype(jnp.float32),
    )
    down_fetched = down_fetched.astype(jnp.bfloat16)
    up_fetched = up_fetched.astype(jnp.bfloat16)
    block_rows = lax.all_gather(modulated, "adapt", axis=0, tiled=True)
    shrunk = jnp.einsum(
        "rtd,rdk->rtk", block_rows, down_fetched, preferred_element_type=jnp.float32
    ).astype(jnp.bfloat16)
    frozen = jnp.einsum(
        "rtd,dc->rtc", block_rows, query_key_value_weight, preferred_element_type=jnp.float32
    )
    qkv = frozen + jnp.einsum(
        "rtk,rkc->rtc", shrunk, up_fetched, preferred_element_type=jnp.float32
    )
    token_local = qkv.shape[1]
    qkv = qkv.reshape(all_requests, token_local, heads_local, 3, HEAD_SIZE)
    queries = rms_scale(qkv[:, :, :, 0], query_key_gain[0]).astype(jnp.bfloat16)
    image_keys = rms_scale(qkv[:, :, :, 1], query_key_gain[1]).astype(jnp.bfloat16)
    image_values = qkv[:, :, :, 2].astype(jnp.bfloat16)
    image_pairs = jnp.transpose(jnp.stack([image_keys, image_values], axis=3), (0, 2, 1, 3, 4))
    text_pairs = jnp.transpose(
        text_key_value.reshape(all_requests, text_local, 2, heads_local, HEAD_SIZE), (0, 3, 1, 2, 4)
    )
    joined = jnp.concatenate([image_pairs, text_pairs], axis=2)
    joined = joined.reshape(all_requests * heads_local, token_local + text_local, 2, HEAD_SIZE)
    queries = jnp.transpose(queries, (0, 2, 1, 3)).reshape(
        all_requests * heads_local, token_local, HEAD_SIZE
    )
    query_items, joined_items = (
        lax.all_to_all(queries, "seq", split_axis=0, concat_axis=1, tiled=True),
        lax.all_to_all(joined, "seq", split_axis=0, concat_axis=1, tiled=True),
    )
    attended = lax.map(attend_item, (query_items, joined_items))
    returned = lax.all_to_all(attended, "seq", split_axis=1, concat_axis=0, tiled=True)
    returned = returned.reshape(all_requests, heads_local, token_local, HEAD_SIZE)
    return jnp.transpose(returned, (0, 2, 1, 3)).reshape(
        all_requests, token_local, heads_local * HEAD_SIZE
    )


def solution(mesh):
    in_specs = (
        P(("groups", "adapt"), "seq", None),
        P(("groups", "adapt"), None, None),
        P(None, "adapt"),
        P("seq", None, None),
        P("seq", None, "adapt"),
        P("groups"),
        P(),
        P("groups"),
        P("groups", "seq", None, "adapt"),
        P(),
    )
    out_specs = P("groups", "seq", "adapt")
    return jax.shard_map(
        on_device, mesh=mesh, in_specs=in_specs, out_specs=out_specs, check_vma=False
    )
```

profile of v0, /device:TPU:0, one launch (start us, length us, event | category | flops | bytes accessed | tf_op | source)
XLA Modules:
  0.0 888.3 jit_solution(3175267230559958143)
XLA Ops:
  9.2 2.8 convolution_convert_fusion
  12.1 3.1 convolution_convert_fusion.1
  15.2 3.7 convert_reduce_fusion
  18.9 4.5 fusion.10
  23.6 9.4 %fusion.13 = bf16[2,512,3072]{2,1,0:T(8,128)(2,1)} fusion(bf16[2,512,3072]{2,1,0:T(8,128)(2,1)} %param.14, f32[2,3072]{1,0:T(2,128)S(1)} %get-tuple-element.83, f32[2,512]{1,0:T(2,128)S(1)} %add_rsqrt_fusion.2, f32[2,512]{1,0:T(2,128)S(1)} %broadcast_multiply_fusion, f32[2,3072]{1,0:T(2,128)S(1)} %get-tuple-element.84), kind=kLoop, calls=%fused_computation.24 | loop fusion | flops 18874368 | bytes 12640256 | tf_op jit(solution)/shard_map/convert_element_type | solution.py:15
  34.2 156.1 %all-reduce.3.cloned.1.call-done = (bf16[8,64,1536]{2,0,1:T(8,128)(2,1)}, bf16[8,3072,64]{1,0,2:T(8,128)(2,1)}) async-done(((bf16[8,64,1536]{2,0,1:T(8,128)(2,1)}, bf16[8,3072,64]{1,0,2:T(8,128)(2,1)}), (bf16[8,64,1536]{2,0,1:T(8,128)(2,1)}, bf16[8,3072,64]{1,0,2:T(8,128)(2,1)})) %all-reduce.3.cloned.1.call-update) | async-done | bytes 4718608 | tf_op jit(solution)/shard_map/psum | solution.py:86
  190.3 23.9 %fusion.18 = f32[8,512,1536]{2,1,0:T(8,128)} fusion(bf16[8,64,1536]{2,0,1:T(8,128)(2,1)} %get-tuple-element.73, bf16[8,512,3072]{2,1,0:T(8,128)(2,1)} %all-gather.2.cloned.1.call-done, bf16[8,3072,64]{1,0,2:T(8,128)(2,1)} %get-tuple-element.74), kind=kOutput, calls=%fused_computation.40 | convolution fusion | flops 2416181248 | bytes 55050240 | tf_op jit(solution)/shard_map/rtk,rkc->rtc/dot_general | solution.py:97
  214.3 47.6 %convolution_add_fusion = f32[8,512,1536]{2,1,0:T(8,128)} fusion(f32[8,512,1536]{2,1,0:T(8,128)} %fusion.18, bf16[8,512,3072]{2,1,0:T(8,128)(2,1)} %all-gather.2.cloned.1.call-done, bf16[3072,1536]{1,0:T(8,128)(2,1)} %param.16), kind=kOutput, calls=%fused_computation.16 | convolution fusion | flops 38660997120 | bytes 84934656 | tf_op jit(solution)/shard_map/rtd,dc->rtc/dot_general | solution.py:94
  261.9 24.7 %copy.49 = f32[8,512,1536]{1,2,0:T(8,128)} copy(f32[8,512,1536]{2,1,0:T(8,128)} %convolution_add_fusion) | data formatting | bytes 50331648 | tf_op jit(solution)/shard_map/add | solution.py:97
  286.6 4.6 multiply_reduce_fusion.1
  291.2 7.0 fusion.15
  298.2 6.5 copy.50
  304.6 5.2 all-to-all-start
  309.8 6.2 copy.52
  316.0 3.2 copy.79
  319.1 4.0 slice.55
  323.1 4.6 multiply_reduce_fusion
  327.8 7.0 multiply_convert_fusion
  334.7 6.2 maximum_bitcast_fusion
  340.9 9.1 %pad_maximum_fusion = bf16[8,4,640,2,128]{2,4,3,1,0:T(8,128)(2,1)} fusion(bf16[8,4,128,2,128]{2,4,3,1,0:T(8,128)(2,1)} %bitcast.102, bf16[8,4,512,2,128]{2,4,3,1,0:T(8,128)(2,1)} %maximum_bitcast_fusion), kind=kLoop, calls=%fused_computation.25 | loop fusion | flops 20971520 | bytes 20971520 | tf_op jit(solution)/shard_map/concatenate | solution.py:109
  350.1 15.1 %copy.54 = bf16[8,4,640,2,128]{4,2,3,1,0:T(8,128)(2,1)} copy(bf16[8,4,640,2,128]{2,4,3,1,0:T(8,128)(2,1)} %pad_maximum_fusion) | data formatting | bytes 20971520 | tf_op jit(solution)/shard_map/concatenate | solution.py:109
  365.2 38.2 %all-to-all-done = bf16[32,512,128]{2,1,0:T(8,128)(2,1)} async-done(((bf16[32,512,128]{2,1,0:T(8,128)(2,1)}), bf16[32,512,128]{2,1,0:T(8,128)(2,1)}, u32[]{:S(2)}, u32[]{:S(2)}) %all-to-all-start) | async-done | bytes 4194336 | tf_op jit(solution)/shard_map/all_to_all | solution.py:115
  403.3 6.0 all-to-all-start.1
  409.4 4.6 copy.51
  414.0 223.2 %all-to-all-done.1 = bf16[32,640,2,128]{3,1,2,0:T(8,128)(2,1)} async-done(((bf16[32,640,2,128]{3,1,2,0:T(8,128)(2,1)}), bf16[32,640,2,128]{3,1,2,0:T(8,128)(2,1)}, u32[]{:S(2)}, u32[]{:S(2)}) %all-to-all-start.1) | async-done | bytes 10485792 | tf_op jit(solution)/shard_map/all_to_all | solution.py:116
  637.1 9.2 %copy.55 = bf16[8,4,640,2,128]{4,2,1,3,0:T(8,128)(2,1)} copy(bf16[8,4,640,2,128]{4,2,3,0,1:T(8,128)(2,1)} %bitcast.23) | data formatting | bytes 20971520 | tf_op jit(solution)/shard_map/all_to_all | solution.py:116
  646.3 118.3 %while.21 = (s32[]{:T(128)}, bf16[8,2048,128]{2,1,0:T(8,128)(2,1)}, bf16[8,2048,128]{2,1,0:T(8,128)(2,1)}, bf16[8,2560,2,128]{3,1,2,0:T(8,128)(2,1)}, s32[]{:T(128)}, /*index=5*/s32[]{:T(128)}, s32[]{:T(128)}) while((s32[]{:T(128)}, bf16[8,2048,128]{2,1,0:T(8,128)(2,1)}, bf16[8,2048,128]{2,1,0:T(8,128)(2,1)}, ...), condition=%wide.region_13.14_spmd, body=%wide.region_8.13_spmd.sunk | while | flops 680328192 | bytes 24652504 | solution.py:118
  646.3 1.4 dynamic-slice_bitcast_fusion.2
  648.9 11.3 %while.22 = (s32[]{:T(128)}, bf16[4,512,128]{2,1,0:T(8,128)(2,1)S(1)}, bf16[4,512,128]{2,1,0:T(8,128)(2,1)S(1)}, bf16[2560,128]{1,0:T(8,128)(2,1)S(1)}, bf16[2560,128]{1,0:T(8,128)(2,1)S(1)}, /*index=5*/s32[]{:T(128)}) while((s32[]{:T(128)}, bf16[4,512,128]{2,1,0:T(8,128)(2,1)S(1)}, bf16[4,512,128]{2,1,0:T(8,128)(2,1)S(1)}, ...), condition=%wide.region_12.12_spmd, body=%wide.region_9.11_spmd.sunk | while | flops 680328192 | bytes 17311820 | solution.py:47
  661.1 1.4 dynamic-slice_bitcast_fusion.2
  663.7 11.4 %while.22 = (s32[]{:T(128)}, bf16[4,512,128]{2,1,0:T(8,128)(2,1)S(1)}, bf16[4,512,128]{2,1,0:T(8,128)(2,1)S(1)}, bf16[2560,128]{1,0:T(8,128)(2,1)S(1)}, bf16[2560,128]{1,0:T(8,128)(2,1)S(1)}, /*index=5*/s32[]{:T(128)}) while((s32[]{:T(128)}, bf16[4,512,128]{2,1,0:T(8,128)(2,1)S(1)}, bf16[4,512,128]{2,1,0:T(8,128)(2,1)S(1)}, ...), condition=%wide.region_12.12_spmd, body=%wide.region_9.11_spmd.sunk | while | flops 680328192 | bytes 17311820 | solution.py:47
  675.9 1.4 dynamic-slice_bitcast_fusion.2
  678.5 11.4 %while.22 = (s32[]{:T(128)}, bf16[4,512,128]{2,1,0:T(8,128)(2,1)S(1)}, bf16[4,512,128]{2,1,0:T(8,128)(2,1)S(1)}, bf16[2560,128]{1,0:T(8,128)(2,1)S(1)}, bf16[2560,128]{1,0:T(8,128)(2,1)S(1)}, /*index=5*/s32[]{:T(128)}) while((s32[]{:T(128)}, bf16[4,512,128]{2,1,0:T(8,128)(2,1)S(1)}, bf16[4,512,128]{2,1,0:T(8,128)(2,1)S(1)}, ...), condition=%wide.region_12.12_spmd, body=%wide.region_9.11_spmd.sunk | while | flops 680328192 | bytes 17311820 | solution.py:47
  690.7 1.4 dynamic-slice_bitcast_fusion.2
  693.3 11.4 %while.22 = (s32[]{:T(128)}, bf16[4,512,128]{2,1,0:T(8,128)(2,1)S(1)}, bf16[4,512,128]{2,1,0:T(8,128)(2,1)S(1)}, bf16[2560,128]{1,0:T(8,128)(2,1)S(1)}, bf16[2560,128]{1,0:T(8,128)(2,1)S(1)}, /*index=5*/s32[]{:T(128)}) while((s32[]{:T(128)}, bf16[4,512,128]{2,1,0:T(8,128)(2,1)S(1)}, bf16[4,512,128]{2,1,0:T(8,128)(2,1)S(1)}, ...), condition=%wide.region_12.12_spmd, body=%wide.region_9.11_spmd.sunk | while | flops 680328192 | bytes 17311820 | solution.py:47
  705.5 1.4 dynamic-slice_bitcast_fusion.2
  708.1 11.4 %while.22 = (s32[]{:T(128)}, bf16[4,512,128]{2,1,0:T(8,128)(2,1)S(1)}, bf16[4,512,128]{2,1,0:T(8,128)(2,1)S(1)}, bf16[2560,128]{1,0:T(8,128)(2,1)S(1)}, bf16[2560,128]{1,0:T(8,128)(2,1)S(1)}, /*index=5*/s32[]{:T(128)}) while((s32[]{:T(128)}, bf16[4,512,128]{2,1,0:T(8,128)(2,1)S(1)}, bf16[4,512,128]{2,1,0:T(8,128)(2,1)S(1)}, ...), condition=%wide.region_12.12_spmd, body=%wide.region_9.11_spmd.sunk | while | flops 680328192 | bytes 17311820 | solution.py:47
  720.3 1.4 dynamic-slice_bitcast_fusion.2
  722.9 11.4 %while.22 = (s32[]{:T(128)}, bf16[4,512,128]{2,1,0:T(8,128)(2,1)S(1)}, bf16[4,512,128]{2,1,0:T(8,128)(2,1)S(1)}, bf16[2560,128]{1,0:T(8,128)(2,1)S(1)}, bf16[2560,128]{1,0:T(8,128)(2,1)S(1)}, /*index=5*/s32[]{:T(128)}) while((s32[]{:T(128)}, bf16[4,512,128]{2,1,0:T(8,128)(2,1)S(1)}, bf16[4,512,128]{2,1,0:T(8,128)(2,1)S(1)}, ...), condition=%wide.region_12.12_spmd, body=%wide.region_9.11_spmd.sunk | while | flops 680328192 | bytes 17311820 | solution.py:47
  735.1 1.4 dynamic-slice_bitcast_fusion.2
  737.6 11.4 %while.22 = (s32[]{:T(128)}, bf16[4,512,128]{2,1,0:T(8,128)(2,1)S(1)}, bf16[4,512,128]{2,1,0:T(8,128)(2,1)S(1)}, bf16[2560,128]{1,0:T(8,128)(2,1)S(1)}, bf16[2560,128]{1,0:T(8,128)(2,1)S(1)}, /*index=5*/s32[]{:T(128)}) while((s32[]{:T(128)}, bf16[4,512,128]{2,1,0:T(8,128)(2,1)S(1)}, bf16[4,512,128]{2,1,0:T(8,128)(2,1)S(1)}, ...), condition=%wide.region_12.12_spmd, body=%wide.region_9.11_spmd.sunk | while | flops 680328192 | bytes 17311820 | solution.py:47
  749.8 1.4 dynamic-slice_bitcast_fusion.2
  752.4 11.4 %while.22 = (s32[]{:T(128)}, bf16[4,512,128]{2,1,0:T(8,128)(2,1)S(1)}, bf16[4,512,128]{2,1,0:T(8,128)(2,1)S(1)}, bf16[2560,128]{1,0:T(8,128)(2,1)S(1)}, bf16[2560,128]{1,0:T(8,128)(2,1)S(1)}, /*index=5*/s32[]{:T(128)}) while((s32[]{:T(128)}, bf16[4,512,128]{2,1,0:T(8,128)(2,1)S(1)}, bf16[4,512,128]{2,1,0:T(8,128)(2,1)S(1)}, ...), condition=%wide.region_12.12_spmd, body=%wide.region_9.11_spmd.sunk | while | flops 680328192 | bytes 17311820 | solution.py:47
  764.6 4.9 copy.56
  769.5 95.4 %all_to_all.51 = bf16[8,2048,128]{2,0,1:T(8,128)(2,1)S(1)} all-to-all(bf16[8,2048,128]{2,0,1:T(8,128)(2,1)S(1)} %copy.56), channel_id=1, replica_groups=mesh['groups'=2,'seq'=4,'adapt'=4] {'seq'}, dimensions={1} | all-to-all | bytes 8388608 | tf_op jit(solution)/shard_map/all_to_all | solution.py:119
  864.9 2.9 copy.58
  867.8 6.6 copy.59
  874.4 6.4 copy.60
  (155 shorter events, 109.5 us)
Async XLA Ops:
  7.4 1.8 copy-start
  7.4 182.9 %all-reduce.3.cloned.1.call-start = ((), (), s32[]{:S(2)}) async-start(), calls=%async_computation.4 | async-start | bytes 9437184 | tf_op jit(solution)/shard_map/psum | solution.py:86
  15.2 8.3 copy-start.2
  15.2 175.1 %all-gather.2.cloned.1.call-start = ((), (), s32[]{:S(2)}) async-start(), calls=%async_computation.3 | async-start | bytes 31457280 | tf_op jit(solution)/shard_map/all_gather | solution.py:90
  33.0 0.7 copy-start.4
  304.6 98.7 %all-to-all-start = ((bf16[32,512,128]{2,1,0:T(8,128)(2,1)}), bf16[32,512,128]{2,1,0:T(8,128)(2,1)}, u32[]{:S(2)}, u32[]{:S(2)}) async-start(bf16[32,512,128]{2,1,0:T(8,128)(2,1)} %bitcast.96), calls=%async_computation | async-start | bytes 8388608 | tf_op jit(solution)/shard_map/all_to_all | solution.py:115
  323.1 4.6 copy-start.3
  403.3 233.8 %all-to-all-start.1 = ((bf16[32,640,2,128]{3,1,2,0:T(8,128)(2,1)}), bf16[32,640,2,128]{3,1,2,0:T(8,128)(2,1)}, u32[]{:S(2)}, u32[]{:S(2)}) async-start(bf16[32,640,2,128]{3,1,2,0:T(8,128)(2,1)} %bitcast.94), calls=%async_computation.1 | async-start | bytes 20971520 | tf_op jit(solution)/shard_map/all_to_all | solution.py:116
  867.8 13.0 %copy-start.1 = (bf16[4,3072,64]{1,2,0:T(8,128)(2,1)S(1)}, bf16[4,3072,64]{1,2,0:T(8,128)(2,1)}, u32[]{:S(2)}) copy-start(bf16[4,3072,64]{1,2,0:T(8,128)(2,1)} %param.17) | copy-start | bytes 4718596
Sparse Core Ops, SparseCore 0:
  15.3 174.9 all-reduce.2
Sparse Core Ops, SparseCore 1:
  33.1 157.0 all-gather.1
where the time goes:
time: 891 us; the launch traced here: 888 us
  waiting for transfers between devices  417 us (47%)
  matrix products  141 us (16%)
  local copies, waits for them, and re-layouts  123 us (14%)
  blocking collectives  95.4 us (11%)
  other arithmetic  85 us (10%)
  between operations  15 us (2%)
  starting transfers between devices  11.2 us (1%)
    all_to_all x1, waiting for transfers between devices, on_device(): lax.all_to_all(joined, 'seq', split_axis=0, concat_axis=1, tiled=True)  223 us
    psum x1, waiting for transfers between devices, on_device(): lax.psum(up_terms, 'seq').astype(jnp.float32)  156 us
    all_to_all x1, blocking collectives, on_device(): lax.all_to_all(attended, 'seq', split_axis=1, concat_axis=0, tiled=True)  95.4 us
    dot_general x1, matrix products, on_device(): jnp.einsum('rtd,dc->rtc', block_rows, query_key_value_weight, preferred_e...  47.6 us
    all_to_all x1, waiting for transfers between devices, on_device(): lax.all_to_all(queries, 'seq', split_axis=0, concat_axis=1, tiled=True)  38.2 us
    dot_general x32, matrix products, one_block(): jnp.dot(weights.astype(jnp.bfloat16), value_rows, preferred_element_type=...  33.5 us
    dot_general x32, matrix products, one_block(): lax.dot_general(block_rows, key_rows, (((1,), (1,)), ((), ())), preferred...  29.7 us
    reduce_sum x32, other arithmetic, one_block(): weights = weights / jnp.sum(weights, axis=-1, keepdims=True)  27 us
  transfers between devices with their start and end apart: 4, of which 3 were waited for; matrix products, arithmetic and copies ran while one was open for 9% of the time, Pallas kernels for 0%

commit v1 on v0

--- a/solution.py
+++ b/solution.py
@@ -5,6 +5,23 @@
 from jax.sharding import PartitionSpec as P
 
 HEAD_SIZE = 128
+
+
+def keep_up_signs_in(arr, where_dim, content):
+    local_out = arr.shape
+    clean = arr.reshape(
+        *local_out[:where_dim],
+        content,
+        local_out[where_dim] // content,
+        *local_out[where_dim + 1 :]
+    )
+    return jnp.moveaxis(clean, where_dim, 0)
+
+
+def _get_teams(q_in, k_dim):
+    q_in = jnp.moveaxis(q_in, 0, k_dim)
+    then = q_in.shape
+    return q_in.reshape(*then[:k_dim], then[k_dim] * then[k_dim + 1], *then[k_dim + 2 :])
 
 
 def layer_modulate(image, modulation):
@@ -111,9 +128,27 @@
     queries = jnp.transpose(queries, (0, 2, 1, 3)).reshape(
         all_requests * heads_local, token_local, HEAD_SIZE
     )
+
+    def apply_the_runs(mesh_ax, t0, local_x, u):
+        part_next = lax.axis_size(mesh_ax)
+        met_up = lax.axis_index(mesh_ax)
+        piece_out, upper = (part_next, met_up)
+        built = keep_up_signs_in(t0, local_x, piece_out)
+        runs = [built[upper]]
+        for rr in [*range(1, piece_out)]:
+            taken_in = built[(upper + rr) % piece_out]
+            runs.append(
+                lax.ppermute(
+                    taken_in, mesh_ax, perm=[(it, (it + rr) % piece_out) for it in range(piece_out)]
+                )
+            )
+        vec_out = jnp.stack(runs)
+        built = vec_out[(upper - jnp.arange(piece_out)) % piece_out]
+        return _get_teams(built, u)
+
     query_items, joined_items = (
         lax.all_to_all(queries, "seq", split_axis=0, concat_axis=1, tiled=True),
-        lax.all_to_all(joined, "seq", split_axis=0, concat_axis=1, tiled=True),
+        apply_the_runs("seq", joined, 0, 1),
     )
     attended = lax.map(attend_item, (query_items, joined_items))
     returned = lax.all_to_all(attended, "seq", split_axis=1, concat_axis=0, tiled=True)

time: 891 us -> 935 us (1.049)
  waiting for transfers between devices: 417 us -> 354 us
  blocking collectives: 95.4 us -> 151 us
  local copies, waits for them, and re-layouts: 123 us -> 146 us
  other arithmetic: 85 us -> 107 us
    all_to_all x1 -> x0, waiting for transfers between devices: 223 us -> none  [on_device(): lax.all_to_all(joined, 'seq', split_axis=0, concat_axis=1, tiled=True)]
    ppermute x0 -> x3, waiting for transfers between devices: none -> 208 us  [apply_the_runs(): lax.ppermute(taken_in, mesh_ax, perm=[(it, (it + rr) % piece_out) for it...]
    all_to_all x1, blocking collectives: 95.4 us -> 151 us  [on_device(): lax.all_to_all(attended, 'seq', split_axis=1, concat_axis=0, tiled=True)]
    all_to_all x1, waiting for transfers between devices: 38.2 us -> 0.01 us  [on_device(): lax.all_to_all(queries, 'seq', split_axis=0, concat_axis=1, tiled=True)]
    gather x0 -> x3, local copies, waits for them, and re-layouts: none -> 15.1 us  [apply_the_runs(): built = vec_out[(upper - jnp.arange(piece_out)) % piece_out]]
    transpose x0 -> x1, other arithmetic: none -> 12.1 us  [_get_teams(): q_in = jnp.moveaxis(q_in, 0, k_dim)]
  transfers between devices with their start and end apart: 4 -> 6, of which waited for: 3 -> 3; matrix products, arithmetic and copies ran while one was open for 9% -> 13% of each run, Pallas kernels for 0% -> 0%
where the time goes in v1:
time: 935 us; the launch traced here: 926 us
  waiting for transfers between devices  354 us (38%)
  blocking collectives  151 us (16%)
  local copies, waits for them, and re-layouts  146 us (16%)
  matrix products  141 us (15%)
  other arithmetic  107 us (11%)
  between operations  15.3 us (2%)
  starting transfers between devices  10.8 us (1%)
    ppermute x3, waiting for transfers between devices, apply_the_runs(): lax.ppermute(taken_in, mesh_ax, perm=[(it, (it + rr) % piece_out) for it...  208 us
    all_to_all x1, blocking collectives, on_device(): lax.all_to_all(attended, 'seq', split_axis=1, concat_axis=0, tiled=True)  151 us
    psum x1, waiting for transfers between devices, on_device(): lax.psum(up_terms, 'seq').astype(jnp.float32)  147 us
    dot_general x1, matrix products, on_device(): jnp.einsum('rtd,dc->rtc', block_rows, query_key_value_weight, preferred_e...  47.6 us
    dot_general x32, matrix products, one_block(): jnp.dot(weights.astype(jnp.bfloat16), value_rows, preferred_element_type=...  33.5 us
    dot_general x32, matrix products, one_block(): lax.dot_general(block_rows, key_rows, (((1,), (1,)), ((), ())), preferred...  29.7 us
    reduce_sum x32, other arithmetic, one_block(): weights = weights / jnp.sum(weights, axis=-1, keepdims=True)  27 us
    add x1, local copies, waits for them, and re-layouts, on_device(): frozen + jnp.einsum('rtk,rkc->rtc', shrunk, up_fetched, preferred_element...  24.8 us
  transfers between devices with their start and end apart: 6, of which 3 were waited for; matrix products, arithmetic and copies ran while one was open for 13% of the time, Pallas kernels for 0%

profile of v1, /device:TPU:0, one launch (start us, length us, event | category | flops | bytes accessed | tf_op | source)
XLA Modules:
  0.0 926.0 jit_solution(8158428505150302863)
XLA Ops:
  9.2 2.8 convolution_convert_fusion
  12.1 3.1 convolution_convert_fusion.1
  15.2 3.7 convert_reduce_fusion
  18.9 4.5 fusion.10
  23.6 9.4 %fusion.13 = bf16[2,512,3072]{2,1,0:T(8,128)(2,1)} fusion(bf16[2,512,3072]{2,1,0:T(8,128)(2,1)} %param.14, f32[2,3072]{1,0:T(2,128)S(1)} %get-tuple-element.87, f32[2,512]{1,0:T(2,128)S(1)} %add_rsqrt_fusion.2, f32[2,512]{1,0:T(2,128)S(1)} %broadcast_multiply_fusion, f32[2,3072]{1,0:T(2,128)S(1)} %get-tuple-element.88), kind=kLoop, calls=%fused_computation.26 | loop fusion | flops 18874368 | bytes 12640256 | tf_op jit(solution)/shard_map/convert_element_type | solution.py:32
  33.0 6.6 copy.52
  39.7 3.2 copy.79
  43.4 146.9 %all-reduce.3.cloned.1.call-done = (bf16[8,64,1536]{2,0,1:T(8,128)(2,1)}, bf16[8,3072,64]{1,0,2:T(8,128)(2,1)}) async-done(((bf16[8,64,1536]{2,0,1:T(8,128)(2,1)}, bf16[8,3072,64]{1,0,2:T(8,128)(2,1)}), (bf16[8,64,1536]{2,0,1:T(8,128)(2,1)}, bf16[8,3072,64]{1,0,2:T(8,128)(2,1)})) %all-reduce.3.cloned.1.call-update) | async-done | bytes 4718608 | tf_op jit(solution)/shard_map/psum | solution.py:103
  190.3 23.9 %fusion.18 = f32[8,512,1536]{2,1,0:T(8,128)} fusion(bf16[8,64,1536]{2,0,1:T(8,128)(2,1)} %get-tuple-element.73, bf16[8,512,3072]{2,1,0:T(8,128)(2,1)} %all-gather.2.cloned.1.call-done, bf16[8,3072,64]{1,0,2:T(8,128)(2,1)} %get-tuple-element.74), kind=kOutput, calls=%fused_computation.48 | convolution fusion | flops 2416181248 | bytes 55050240 | tf_op jit(solution)/shard_map/rtk,rkc->rtc/dot_general | solution.py:114
  214.2 47.6 %convolution_add_fusion = f32[8,512,1536]{2,1,0:T(8,128)} fusion(f32[8,512,1536]{2,1,0:T(8,128)} %fusion.18, bf16[8,512,3072]{2,1,0:T(8,128)(2,1)} %all-gather.2.cloned.1.call-done, bf16[3072,1536]{1,0:T(8,128)(2,1)} %param.16), kind=kOutput, calls=%fused_computation.18 | convolution fusion | flops 38660997120 | bytes 84934656 | tf_op jit(solution)/shard_map/rtd,dc->rtc/dot_general | solution.py:111
  261.8 24.8 %copy.49 = f32[8,512,1536]{1,2,0:T(8,128)} copy(f32[8,512,1536]{2,1,0:T(8,128)} %convolution_add_fusion) | data formatting | bytes 50331648 | tf_op jit(solution)/shard_map/add | solution.py:114
  286.7 4.6 multiply_reduce_fusion
  291.2 4.6 multiply_reduce_fusion.1
  295.8 7.0 fusion.15
  302.8 6.5 copy.50
  309.3 4.9 all-to-all-start
  314.3 4.0 slice.59
  318.3 7.0 multiply_convert_fusion
  325.3 6.2 maximum_bitcast_fusion.1
  331.5 9.1 pad_maximum_fusion
  340.6 15.1 %copy.54 = bf16[8,4,640,2,128]{4,2,3,1,0:T(8,128)(2,1)} copy(bf16[8,4,640,2,128]{2,4,3,1,0:T(8,128)(2,1)} %pad_maximum_fusion) | data formatting | bytes 20971520 | tf_op jit(solution)/shard_map/concatenate | solution.py:126
  355.7 8.3 constant_dynamic-slice_fusion.1
  364.0 2.0 collective-permute-start
  366.0 2.4 collective-permute-start.1
  369.8 73.8 %collective-permute-done = bf16[8,640,2,128]{3,1,2,0:T(8,128)(2,1)} collective-permute-done((bf16[8,640,2,128]{3,1,2,0:T(8,128)(2,1)}, bf16[8,640,2,128]{3,1,2,0:T(8,128)(2,1)}, u32[]{:S(2)}, u32[]{:S(2)}) %collective-permute-start) | collective-permute-done | bytes 2621472 | tf_op jit(solution)/shard_map/ppermute | solution.py:141
  443.6 133.8 %collective-permute-done.1 = bf16[8,640,2,128]{3,1,2,0:T(8,128)(2,1)} collective-permute-done((bf16[8,640,2,128]{3,1,2,0:T(8,128)(2,1)}, bf16[8,640,2,128]{3,1,2,0:T(8,128)(2,1)}, u32[]{:S(2)}, u32[]{:S(2)}) %collective-permute-start.1) | collective-permute-done | bytes 2621472 | tf_op jit(solution)/shard_map/ppermute | solution.py:141
  577.4 5.8 pad_maximum_fusion.1
  583.2 3.1 mini-gather-slice.2
  586.2 6.8 gather_fusion
  593.0 4.1 pad_maximum_fusion.2
  597.2 5.2 gather_fusion.1
  602.4 12.1 %maximum_bitcast_fusion = bf16[8,4,640,2,128]{4,2,3,0,1:T(8,128)(2,1)} fusion(bf16[4,8,256,2,128]{4,2,3,1,0:T(8,128)(2,1)} %gather_fusion.1, bf16[4,8,384,2,128]{4,2,3,1,0:T(8,128)(2,1)} %gather_fusion), kind=kLoop, calls=%fused_computation.29 | loop fusion | flops 20971520 | bytes 20971520 | tf_op jit(solution)/shard_map/transpose | solution.py:22
  614.5 9.2 copy.55
  623.7 4.7 copy.51
  628.4 118.3 %while.21 = (s32[]{:T(128)}, bf16[8,2048,128]{2,1,0:T(8,128)(2,1)}, bf16[8,2048,128]{2,1,0:T(8,128)(2,1)}, bf16[8,2560,2,128]{3,1,2,0:T(8,128)(2,1)}, s32[]{:T(128)}, /*index=5*/s32[]{:T(128)}, s32[]{:T(128)}) while((s32[]{:T(128)}, bf16[8,2048,128]{2,1,0:T(8,128)(2,1)}, bf16[8,2048,128]{2,1,0:T(8,128)(2,1)}, ...), condition=%wide.region_13.14_spmd, body=%wide.region_8.13_spmd.sunk | while | flops 680328192 | bytes 24652504 | solution.py:153
  631.0 11.4 %while.22 = (s32[]{:T(128)}, bf16[4,512,128]{2,1,0:T(8,128)(2,1)S(1)}, bf16[4,512,128]{2,1,0:T(8,128)(2,1)S(1)}, bf16[2560,128]{1,0:T(8,128)(2,1)S(1)}, bf16[2560,128]{1,0:T(8,128)(2,1)S(1)}, /*index=5*/s32[]{:T(128)}) while((s32[]{:T(128)}, bf16[4,512,128]{2,1,0:T(8,128)(2,1)S(1)}, bf16[4,512,128]{2,1,0:T(8,128)(2,1)S(1)}, ...), condition=%wide.region_12.12_spmd, body=%wide.region_9.11_spmd.sunk | while | flops 680328192 | bytes 17311820 | solution.py:64
  645.8 11.4 %while.22 = (s32[]{:T(128)}, bf16[4,512,128]{2,1,0:T(8,128)(2,1)S(1)}, bf16[4,512,128]{2,1,0:T(8,128)(2,1)S(1)}, bf16[2560,128]{1,0:T(8,128)(2,1)S(1)}, bf16[2560,128]{1,0:T(8,128)(2,1)S(1)}, /*index=5*/s32[]{:T(128)}) while((s32[]{:T(128)}, bf16[4,512,128]{2,1,0:T(8,128)(2,1)S(1)}, bf16[4,512,128]{2,1,0:T(8,128)(2,1)S(1)}, ...), condition=%wide.region_12.12_spmd, body=%wide.region_9.11_spmd.sunk | while | flops 680328192 | bytes 17311820 | solution.py:64
  660.6 11.4 %while.22 = (s32[]{:T(128)}, bf16[4,512,128]{2,1,0:T(8,128)(2,1)S(1)}, bf16[4,512,128]{2,1,0:T(8,128)(2,1)S(1)}, bf16[2560,128]{1,0:T(8,128)(2,1)S(1)}, bf16[2560,128]{1,0:T(8,128)(2,1)S(1)}, /*index=5*/s32[]{:T(128)}) while((s32[]{:T(128)}, bf16[4,512,128]{2,1,0:T(8,128)(2,1)S(1)}, bf16[4,512,128]{2,1,0:T(8,128)(2,1)S(1)}, ...), condition=%wide.region_12.12_spmd, body=%wide.region_9.11_spmd.sunk | while | flops 680328192 | bytes 17311820 | solution.py:64
  675.4 11.4 %while.22 = (s32[]{:T(128)}, bf16[4,512,128]{2,1,0:T(8,128)(2,1)S(1)}, bf16[4,512,128]{2,1,0:T(8,128)(2,1)S(1)}, bf16[2560,128]{1,0:T(8,128)(2,1)S(1)}, bf16[2560,128]{1,0:T(8,128)(2,1)S(1)}, /*index=5*/s32[]{:T(128)}) while((s32[]{:T(128)}, bf16[4,512,128]{2,1,0:T(8,128)(2,1)S(1)}, bf16[4,512,128]{2,1,0:T(8,128)(2,1)S(1)}, ...), condition=%wide.region_12.12_spmd, body=%wide.region_9.11_spmd.sunk | while | flops 680328192 | bytes 17311820 | solution.py:64
  690.2 11.4 %while.22 = (s32[]{:T(128)}, bf16[4,512,128]{2,1,0:T(8,128)(2,1)S(1)}, bf16[4,512,128]{2,1,0:T(8,128)(2,1)S(1)}, bf16[2560,128]{1,0:T(8,128)(2,1)S(1)}, bf16[2560,128]{1,0:T(8,128)(2,1)S(1)}, /*index=5*/s32[]{:T(128)}) while((s32[]{:T(128)}, bf16[4,512,128]{2,1,0:T(8,128)(2,1)S(1)}, bf16[4,512,128]{2,1,0:T(8,128)(2,1)S(1)}, ...), condition=%wide.region_12.12_spmd, body=%wide.region_9.11_spmd.sunk | while | flops 680328192 | bytes 17311820 | solution.py:64
  705.0 11.4 %while.22 = (s32[]{:T(128)}, bf16[4,512,128]{2,1,0:T(8,128)(2,1)S(1)}, bf16[4,512,128]{2,1,0:T(8,128)(2,1)S(1)}, bf16[2560,128]{1,0:T(8,128)(2,1)S(1)}, bf16[2560,128]{1,0:T(8,128)(2,1)S(1)}, /*index=5*/s32[]{:T(128)}) while((s32[]{:T(128)}, bf16[4,512,128]{2,1,0:T(8,128)(2,1)S(1)}, bf16[4,512,128]{2,1,0:T(8,128)(2,1)S(1)}, ...), condition=%wide.region_12.12_spmd, body=%wide.region_9.11_spmd.sunk | while | flops 680328192 | bytes 17311820 | solution.py:64
  719.8 11.4 %while.22 = (s32[]{:T(128)}, bf16[4,512,128]{2,1,0:T(8,128)(2,1)S(1)}, bf16[4,512,128]{2,1,0:T(8,128)(2,1)S(1)}, bf16[2560,128]{1,0:T(8,128)(2,1)S(1)}, bf16[2560,128]{1,0:T(8,128)(2,1)S(1)}, /*index=5*/s32[]{:T(128)}) while((s32[]{:T(128)}, bf16[4,512,128]{2,1,0:T(8,128)(2,1)S(1)}, bf16[4,512,128]{2,1,0:T(8,128)(2,1)S(1)}, ...), condition=%wide.region_12.12_spmd, body=%wide.region_9.11_spmd.sunk | while | flops 680328192 | bytes 17311820 | solution.py:64
  734.5 11.4 %while.22 = (s32[]{:T(128)}, bf16[4,512,128]{2,1,0:T(8,128)(2,1)S(1)}, bf16[4,512,128]{2,1,0:T(8,128)(2,1)S(1)}, bf16[2560,128]{1,0:T(8,128)(2,1)S(1)}, bf16[2560,128]{1,0:T(8,128)(2,1)S(1)}, /*index=5*/s32[]{:T(128)}) while((s32[]{:T(128)}, bf16[4,512,128]{2,1,0:T(8,128)(2,1)S(1)}, bf16[4,512,128]{2,1,0:T(8,128)(2,1)S(1)}, ...), condition=%wide.region_12.12_spmd, body=%wide.region_9.11_spmd.sunk | while | flops 680328192 | bytes 17311820 | solution.py:64
  746.7 4.9 copy.56
  751.6 150.7 %all_to_all.33 = bf16[8,2048,128]{2,0,1:T(8,128)(2,1)S(1)} all-to-all(bf16[8,2048,128]{2,0,1:T(8,128)(2,1)S(1)} %copy.56), channel_id=1, replica_groups=mesh['groups'=2,'seq'=4,'adapt'=4] {'seq'}, dimensions={1} | all-to-all | bytes 8388608 | tf_op jit(solution)/shard_map/all_to_all | solution.py:154
  902.3 2.9 copy.58
  905.3 6.6 copy.59
  911.9 6.4 copy.60
  (168 shorter events, 121.5 us)
Async XLA Ops:
  7.4 1.8 copy-start
  7.4 182.9 %all-reduce.3.cloned.1.call-start = ((), (), s32[]{:S(2)}) async-start(), calls=%async_computation.3 | async-start | bytes 9437184 | tf_op jit(solution)/shard_map/psum | solution.py:103
  15.1 8.3 copy-start.2
  15.2 175.1 %all-gather.2.cloned.1.call-start = ((), (), s32[]{:S(2)}) async-start(), calls=%async_computation.2 | async-start | bytes 31457280 | tf_op jit(solution)/shard_map/all_gather | solution.py:107
  33.0 10.0 %copy-start.4 = (f32[2,128]{1,0:T(2,128)S(1)}, f32[2,128]{1,0:T(2,128)}, u32[]{:S(2)}) copy-start(f32[2,128]{1,0:T(2,128)} %param.23) | copy-start | bytes 3076
  309.3 314.4 %all-to-all-start = ((bf16[32,512,128]{2,1,0:T(8,128)(2,1)}), bf16[32,512,128]{2,1,0:T(8,128)(2,1)}, u32[]{:S(2)}, u32[]{:S(2)}) async-start(bf16[32,512,128]{2,1,0:T(8,128)(2,1)} %bitcast.106), calls=%async_computation | async-start | bytes 8388608 | tf_op jit(solution)/shard_map/all_to_all | solution.py:150
  314.2 4.1 copy-start.3
  364.0 79.6 %collective-permute-start = (bf16[8,640,2,128]{3,1,2,0:T(8,128)(2,1)}, bf16[8,640,2,128]{3,1,2,0:T(8,128)(2,1)}, u32[]{:S(2)}, u32[]{:S(2)}) collective-permute-start(bf16[8,640,2,128]{3,1,2,0:T(8,128)(2,1)} %get-tuple-element.82), channel_id=1, source_target_pairs={{0,4},{4,8},{8,12},{12,0},{1,5},{5,9},{9,13},{13,1},{2,6},{6,10},{... | collective-permute-start | bytes 7864328 | tf_op jit(solution)/shard_map/ppermute | solution.py:141
  366.0 211.4 %collective-permute-start.1 = (bf16[8,640,2,128]{3,1,2,0:T(8,128)(2,1)}, bf16[8,640,2,128]{3,1,2,0:T(8,128)(2,1)}, u32[]{:S(2)}, u32[]{:S(2)}) collective-permute-start(bf16[8,640,2,128]{3,1,2,0:T(8,128)(2,1)} %get-tuple-element.81), channel_id=1, source_target_pairs={{0,8},{4,12},{8,0},{12,4},{1,9},{5,13},{9,1},{13,5},{2,10},{6,14},... | collective-permute-start | bytes 7864328 | tf_op jit(solution)/shard_map/ppermute | solution.py:141
  368.3 209.1 %collective-permute-start.2 = (bf16[8,640,2,128]{3,1,2,0:T(8,128)(2,1)}, bf16[8,640,2,128]{3,1,2,0:T(8,128)(2,1)}, u32[]{:S(2)}, u32[]{:S(2)}) collective-permute-start(bf16[8,640,2,128]{3,1,2,0:T(8,128)(2,1)} %get-tuple-element.80), channel_id=1, source_target_pairs={{0,12},{4,0},{8,4},{12,8},{1,13},{5,1},{9,5},{13,9},{2,14},{6,2},{... | collective-permute-start | bytes 7864328 | tf_op jit(solution)/shard_map/ppermute | solution.py:141
  905.3 13.0 %copy-start.1 = (bf16[4,3072,64]{1,2,0:T(8,128)(2,1)S(1)}, bf16[4,3072,64]{1,2,0:T(8,128)(2,1)}, u32[]{:S(2)}) copy-start(bf16[4,3072,64]{1,2,0:T(8,128)(2,1)} %param.17) | copy-start | bytes 4718596
Sparse Core Ops, SparseCore 0:
  15.3 174.9 all-reduce.2
Sparse Core Ops, SparseCore 1:
  33.1 157.0 all-gather.1
